TPU v7x, 128 devices: a whole 4x4x4 slice. The times are simulated.
128 devices in a mesh: row: 4 (over x), col: 32 (over y, z, core).
Axes of the slice: x: 4, y: 4, z: 4, core: 2. Of those that a mesh axis runs over, the one named last changes fastest.
Arguments:
- node_states: bfloat16 [12288, 512], P(('row', 'col')), may hold values from -6 to 6
- walk_nodes: int32 [1024, 64], P(('row', 'col')), may hold values from 0 to 12287, as said below
- walk_lengths: int32 [1024], P(('row', 'col')), may hold values from 16 to 64
- adjacency: int32 [12288, 12288], P('col', 'row'), may hold values 0 or 1
- w_xz: bfloat16 [2, 512, 2048], replicated, may hold values from -0.25 to 0.25
- w_bc: bfloat16 [2, 512, 256], replicated, may hold values from -0.25 to 0.25
- w_dt: bfloat16 [2, 512, 16], replicated, may hold values from -0.25 to 0.25
- decay_rate: float32 [2, 16], replicated, may hold values from 0.01 to 1
- w_out: bfloat16 [2, 1024, 512], replicated, may hold values from -0.1875 to 0.1875
- w_up: bfloat16 [512, 1024], replicated, may hold values from -0.25 to 0.25
- w_down: bfloat16 [1024, 512], replicated, may hold values from -0.1875 to 0.1875
Outputs:
- refreshed: bfloat16 [12288, 512], P('col')
Inputs may be any that keep to these rules, and one draw needn't show every extreme that they name: `walk_nodes`: among the 8 walks of one device (aligned blocks of walks), at most 8 positions, live or not, fall on the 96 nodes held by any one device (nodes n with the same n // 96).
All inputs are finite; a program needn't handle non-finite values. No bound on the sum of `adjacency` on one device may be relied on, other than what follows from the above.
Results may differ from a plain program's by a relative error of at most 0.018.
Values may be sent and summed in bfloat16 or wider, within the bound.
No kernel may reach another device: no remote copies, remote signals or barrier semaphores. Data moves between devices by JAX's collectives and lax.ppermute only.
A program may use at most 128 MiB of HBM per device.

v0:
```python
import jax
import jax.numpy as jnp
from jax import lax
from jax.sharding import PartitionSpec as P


def encode_walks(first, live, w_xz, w_bc, w_dt, decay_rate, w_out):
    walk_count, walk_len, width = first.shape
    inner_width = w_out.shape[1]
    heads = w_dt.shape[2]
    state_width = w_bc.shape[2] // 2
    head_width = inner_width // heads
    live_mask = live.astype(jnp.float32)
    position_ids = jnp.arange(walk_len, dtype=jnp.int32)
    forward_tri = position_ids[:, None] >= position_ids[None, :]
    backward_tri = position_ids[:, None] <= position_ids[None, :]
    stream = first.reshape(walk_count * walk_len, width)
    for layer_index in range(w_xz.shape[0]):
        widened = stream.astype(jnp.float32)
        normed = (
            widened * lax.rsqrt(jnp.mean(widened * widened, axis=-1, keepdims=True) + 1e-05)
        ).astype(jnp.bfloat16)
        both = jnp.dot(normed, w_xz[layer_index], preferred_element_type=jnp.float32)
        inner = (
            both[:, :inner_width]
            .astype(jnp.bfloat16)
            .reshape(walk_count, walk_len, heads, head_width)
        )
        gate = both[:, inner_width:]
        proj = jnp.dot(normed, w_bc[layer_index], preferred_element_type=jnp.float32).astype(
            jnp.bfloat16
        )
        proj = proj.reshape(walk_count, walk_len, 2 * state_width)
        b_input = proj[..., :state_width]
        c_output = proj[..., state_width:]
        step_size = jax.nn.softplus(
            jnp.dot(normed, w_dt[layer_index], preferred_element_type=jnp.float32)
        )
        step_size = step_size.reshape(walk_count, walk_len, heads)
        log_decay = -decay_rate[layer_index][None, None, :] * step_size
        running = jnp.transpose(jnp.cumsum(log_decay, axis=1), (0, 2, 1))
        before = running - jnp.transpose(log_decay, (0, 2, 1))
        forward_gap = running[:, :, :, None] - running[:, :, None, :]
        backward_gap = before[:, :, None, :] - before[:, :, :, None]
        decay_mat = jnp.where(forward_tri, jnp.exp(jnp.minimum(forward_gap, 0.0)), 0.0)
        decay_mat = decay_mat + jnp.where(
            backward_tri, jnp.exp(jnp.minimum(backward_gap, 0.0)), 0.0
        )
        scores = jnp.einsum(
            "wtk,wsk->wts", c_output, b_input, preferred_element_type=jnp.float32
        ) * state_width ** (-0.5)
        source = jnp.transpose(step_size * live_mask[:, :, None], (0, 2, 1))
        mix = (scores[:, None, :, :] * decay_mat * source[:, :, None, :]).astype(jnp.bfloat16)
        mixed = jnp.einsum("whts,wshp->wthp", mix, inner, preferred_element_type=jnp.float32)
        mixed = mixed.reshape(walk_count * walk_len, inner_width)
        gated = (mixed * jax.nn.silu(gate)).astype(jnp.bfloat16)
        stream = (
            widened + jnp.dot(gated, w_out[layer_index], preferred_element_type=jnp.float32)
        ).astype(jnp.bfloat16)
    return stream


def finish_nodes(combined, w_up, w_down):
    centred = combined - jnp.mean(combined, axis=-1, keepdims=True)
    normal = centred * lax.rsqrt(jnp.mean(centred * centred, axis=-1, keepdims=True) + 1e-05)
    hidden = jax.nn.gelu(
        jnp.dot(normal.astype(jnp.bfloat16), w_up, preferred_element_type=jnp.float32)
    ).astype(jnp.bfloat16)
    return (normal + jnp.dot(hidden, w_down, preferred_element_type=jnp.float32)).astype(
        jnp.bfloat16
    )


def pick_rows(node_states, requests):
    found = requests >= 0
    chosen = node_states[jnp.maximum(requests, 0)]
    return jnp.where(found[:, :, None], chosen, jnp.zeros((), jnp.bfloat16))


def per_device(
    node_states,
    walk_nodes,
    walk_lengths,
    adjacency,
    w_xz,
    w_bc,
    w_dt,
    decay_rate,
    w_out,
    w_up,
    w_down,
):
    node_count, width = node_states.shape
    walk_count, walk_len = walk_nodes.shape
    devices_all = lax.axis_size(("row", "col"))
    tok_count = walk_count * walk_len
    capacity = max(2, 2 * tok_count // devices_all)
    position_ids = jnp.arange(walk_len, dtype=jnp.int32)
    live = position_ids[None, :] < walk_lengths[:, None]
    flat_nodes = walk_nodes.reshape(tok_count)
    flat_live = live.reshape(tok_count)
    owner_ids = flat_nodes // node_count
    local_ids = flat_nodes - owner_ids * node_count
    token_ids = jnp.arange(tok_count, dtype=jnp.int32)
    ordering = jnp.argsort(owner_ids * tok_count + token_ids)
    owner_sorted = owner_ids[ordering]
    owner_range = jnp.arange(devices_all, dtype=jnp.int32)
    per_owner = jnp.sum((owner_ids[:, None] == owner_range[None, :]).astype(jnp.int32), axis=0)
    starts = jnp.cumsum(per_owner) - per_owner
    rank_sorted = token_ids - starts[owner_sorted]
    slot_ids = (
        jnp.zeros((tok_count,), jnp.int32).at[ordering].set(owner_sorted * capacity + rank_sorted)
    )
    wanted = (
        jnp.full((devices_all * capacity,), -1, jnp.int32)
        .at[slot_ids]
        .set(jnp.where(flat_live, local_ids, -1))
    )
    requests = lax.all_to_all(
        wanted.reshape(devices_all, capacity),
        ("row", "col"),
        split_axis=0,
        concat_axis=0,
        tiled=True,
    )
    picked = pick_rows(node_states, requests)
    arrived = lax.all_to_all(picked, ("row", "col"), split_axis=0, concat_axis=0, tiled=True)
    first = arrived.reshape(devices_all * capacity, width)[slot_ids]
    encoded = encode_walks(
        first.reshape(walk_count, walk_len, width), live, w_xz, w_bc, w_dt, decay_rate, w_out
    )
    kept = jnp.where(flat_live[:, None], encoded, jnp.zeros((), jnp.bfloat16))
    outgoing = jnp.zeros((devices_all * capacity, width), jnp.bfloat16).at[slot_ids].set(kept)
    returned = lax.all_to_all(
        outgoing.reshape(devices_all, capacity, width),
        ("row", "col"),
        split_axis=0,
        concat_axis=0,
        tiled=True,
    )
    returned = returned.reshape(devices_all * capacity, width)
    flat_requests = requests.reshape(devices_all * capacity)
    member = flat_requests[None, :] == jnp.arange(node_count, dtype=jnp.int32)[:, None]
    visit_sum = jnp.dot(member.astype(jnp.bfloat16), returned, preferred_element_type=jnp.float32)
    visit_count = jnp.sum(member.astype(jnp.float32), axis=1)
    update = (node_states.astype(jnp.float32) + visit_sum / (1.0 + visit_count)[:, None]).astype(
        jnp.bfloat16
    )
    row_block = adjacency.shape[0]
    row_begin = lax.axis_index("col") * row_block
    col_begin = lax.axis_index("row") * adjacency.shape[1]
    row_global = row_begin + jnp.arange(row_block, dtype=jnp.int32)
    piece = lax.all_gather(update, "col", axis=0, tiled=True)
    piece_rows = piece.shape[0]
    col_global = col_begin + jnp.arange(piece_rows, dtype=jnp.int32)
    self_link = (row_global[:, None] == col_global[None, :]).astype(jnp.int32)
    links = (adjacency + self_link).astype(jnp.bfloat16)
    neighbour_sum = jnp.dot(links, piece, preferred_element_type=jnp.float32)
    combined = lax.psum(neighbour_sum.astype(jnp.bfloat16), "row").astype(jnp.float32)
    return finish_nodes(combined, w_up, w_down)


def solution(mesh):
    return jax.shard_map(
        per_device,
        mesh=mesh,
        in_specs=(
            P(("row", "col"), None),
            P(("row", "col"), None),
            P(("row", "col")),
            P("col", "row"),
            P(),
            P(),
            P(),
            P(),
            P(),
            P(),
            P(),
        ),
        out_specs=P("col", None),
        check_vma=False,
    )
```

profile of v0, /device:TPU:0, one launch (start us, length us, event | category | flops | bytes accessed | tf_op | source)
XLA Modules:
  0.0 278.1 jit_solution(1807728623535561800)
XLA Ops:
  8.4 3.8 %sort.17 = (s32[512]{0:T(512)}, s32[512]{0:T(512)S(1)}) sort(s32[512]{0:T(512)S(1)} %iota_add_fusion.1, s32[512]{0:T(512)S(1)} %iota.44), dimensions={0}, to_apply=%region_0.1 | sort | flops 4608 | bytes 8192 | tf_op jit(solution)/shard_map/jit(argsort)/sort | solution.py:105
  12.2 3.5 %gather_fusion = s32[512]{0:T(512)S(1)} fusion(s32[512]{0:T(512)S(1)} %get-tuple-element.8, s32[1024]{0:T(1024)S(1)} %pad_clamp_fusion.2), kind=kCustom, calls=%fused_computation | custom fusion | bytes 6144 | tf_op jit(solution)/shard_map/gather | solution.py:106
  16.1 3.3 %gather_fusion.1 = s32[512]{0:T(512)S(1)} fusion(s32[128]{0:T(128)S(1)} %sub.82, s32[1024]{0:T(1024)S(1)} %pad_clamp_fusion.1), kind=kCustom, calls=%fused_computation.1 | custom fusion | bytes 6144 | tf_op jit(solution)/shard_map/gather | solution.py:110
  24.5 20.5 %all_to_all.19 = s32[128,1,8]{2,1,0:T(1,128)S(1)} all-to-all(s32[128,1,8]{2,1,0:T(1,128)S(1)} %bitcast.84), channel_id=1, replica_groups=mesh['row'=4,'col'=32] {'row','col'}, dimensions={0} | all-to-all | bytes 8192 | tf_op jit(solution)/shard_map/all_to_all | solution.py:119
  45.4 4.0 %gather_fusion.2 = bf16[1024,512]{1,0:T(8,128)(2,1)S(1)} fusion(bf16[96,512]{1,0:T(8,128)(2,1)S(1)} %copy-done.1, s32[1024]{0:T(1024)S(1)} %broadcast_clamp_fusion), kind=kCustom, calls=%fused_computation.2 | custom fusion | bytes 2101248 | tf_op jit(solution)/shard_map/gather | solution.py:76
  50.6 4.8 %all-to-all-start.1 = ((bf16[128,8,512]{2,1,0:T(8,128)(2,1)}), bf16[128,8,512]{2,1,0:T(8,128)(2,1)S(1)}, u32[]{:S(2)}, u32[]{:S(2)}) async-start(bf16[128,8,512]{2,1,0:T(8,128)(2,1)} %bitcast_select_fusion), calls=%async_computation.1 | async-start | bytes 2097152 | tf_op jit(solution)/shard_map/all_to_all | solution.py:127
  55.5 19.1 %all-to-all-done.1 = bf16[128,8,512]{2,1,0:T(8,128)(2,1)S(1)} async-done(((bf16[128,8,512]{2,1,0:T(8,128)(2,1)}), bf16[128,8,512]{2,1,0:T(8,128)(2,1)S(1)}, u32[]{:S(2)}, u32[]{:S(2)}) %all-to-all-start.1) | async-done | bytes 1048608 | tf_op jit(solution)/shard_map/all_to_all | solution.py:127
  77.5 6.3 %fusion.112 = f32[8,64,16]{2,0,1:T(8,128)S(1)} fusion(f32[8,64,16]{2,0,1:T(8,128)S(1)} %copy.147), kind=kOutput, calls=%fused_computation.165 | output fusion | flops 516096 | bytes 65536 | tf_op jit(solution)/shard_map/jit(cumsum)/reduce_window_sum | solution.py:41
  92.9 6.4 %convolution_bitcast_fusion.1 = f32[8,64,16,64]{1,3,2,0:T(8,128)} fusion(bf16[8,64,16,64]{3,2,1,0:T(8,128)(2,1)} %reshape.227, f32[8,16,64]{2,1,0:T(8,128)S(1)} %copy.149, f32[8,16,64]{2,1,0:T(8,128)S(1)} %bitcast_subtract_fusion.1, f32[8,16,64]{2,1,0:T(8,128)S(1)} %bitcast.80, f32[8,64,64]{2,1,0:T(8,128)S(1)} %convolution_multiply_fusion.1, ...), kind=kOutput, calls=%fused_computation.15 | convolution fusion | flops 72351744 | bytes 3383296 | tf_op jit(solution)/shard_map/whts,wshp->wthp/dot_general | solution.py:54
  99.3 5.6 %copy.151 = f32[8,64,16,64]{3,2,1,0:T(8,128)} copy(f32[8,64,16,64]{1,3,2,0:T(8,128)} %convolution_bitcast_fusion.1) | data formatting | bytes 4194304 | tf_op jit(solution)/shard_map/whts,wshp->wthp/transpose | solution.py:54
  104.9 4.9 %reshape.230 = f32[512,1024]{1,0:T(8,128)} reshape(f32[8,64,16,64]{3,2,1,0:T(8,128)} %copy.151) | data formatting | bytes 4194304 | tf_op jit(solution)/shard_map/reshape | solution.py:55
  109.8 3.6 %fusion.46 = (f32[512]{0:T(512)S(1)}, bf16[512,512]{0,1:T(8,128)(2,1)S(1)}) fusion(bf16[2,1024,512]{2,1,0:T(8,128)(2,1)} %param.19, f32[512,1024]{1,0:T(8,128)} %reshape.230, f32[512,2048]{1,0:T(8,128)} %copy-done.2, bf16[512,512]{0,1:T(8,128)(2,1)S(1)} %copy.145), kind=kOutput, calls=%fused_computation.75 | convolution fusion | flops 541588992 | bytes 6293504 | tf_op jit(solution)/shard_map/dot_general | solution.py:58
  114.3 3.2 %fusion.3 = f32[512,2048]{1,0:T(8,128)} fusion(bf16[2,512,2048]{2,1,0:T(8,128)(2,1)S(1)} %copy-done.3, bf16[512,512]{0,1:T(8,128)(2,1)S(1)} %get-tuple-element.14, f32[512]{0:T(512)S(1)} %add_rsqrt_fusion.1), kind=kOutput, calls=%fused_computation.18 | convolution fusion | flops 1074528256 | bytes 6817792 | tf_op jit(solution)/shard_map/dot_general | solution.py:23
  117.8 6.3 %fusion.113 = f32[8,64,16]{2,0,1:T(8,128)S(1)} fusion(f32[8,64,16]{2,0,1:T(8,128)S(1)} %copy.153), kind=kOutput, calls=%fused_computation.166 | output fusion | flops 516096 | bytes 65536 | tf_op jit(solution)/shard_map/jit(cumsum)/reduce_window_sum | solution.py:41
  128.7 6.4 %convolution_bitcast_fusion = f32[8,64,16,64]{1,3,2,0:T(8,128)} fusion(bf16[8,64,16,64]{3,2,1,0:T(8,128)(2,1)} %reshape.231, f32[8,16,64]{2,1,0:T(8,128)S(1)} %copy.155, f32[8,16,64]{2,1,0:T(8,128)S(1)} %bitcast_subtract_fusion, f32[8,16,64]{2,1,0:T(8,128)S(1)} %bitcast.81, f32[8,64,64]{2,1,0:T(8,128)S(1)} %convolution_multiply_fusion, ...), kind=kOutput, calls=%fused_computation.14 | convolution fusion | flops 72351744 | bytes 3383296 | tf_op jit(solution)/shard_map/whts,wshp->wthp/dot_general | solution.py:54
  135.1 5.6 %copy.157 = f32[8,64,16,64]{3,2,1,0:T(8,128)} copy(f32[8,64,16,64]{1,3,2,0:T(8,128)} %convolution_bitcast_fusion) | data formatting | bytes 4194304 | tf_op jit(solution)/shard_map/whts,wshp->wthp/transpose | solution.py:54
  140.7 3.5 %reshape.234 = f32[512,1024]{1,0:T(8,128)S(1)} reshape(f32[8,64,16,64]{3,2,1,0:T(8,128)} %copy.157) | data formatting | bytes 4194304 | tf_op jit(solution)/shard_map/reshape | solution.py:55
  144.2 3.8 %fusion.41 = bf16[512,512]{0,1:T(8,128)(2,1)} fusion(bf16[512,512]{0,1:T(8,128)(2,1)} %copy-done.4, bf16[2,1024,512]{2,1,0:T(8,128)(2,1)} %param.19, f32[512,1024]{1,0:T(8,128)S(1)} %reshape.234, f32[512,2048]{1,0:T(8,128)} %fusion.3, pred[512]{0:T(512)(128)(4,1)S(1)} %lt.51), kind=kOutput, calls=%fused_computation.65 | convolution fusion | flops 541065216 | bytes 6291968 | tf_op jit(solution)/shard_map/dot_general | solution.py:58
  149.2 3.5 %scatter_custom_fusion.2 = bf16[1024,512]{1,0:T(8,128)(2,1)} fusion(s32[512]{0:T(512)S(1)} %compare_select_fusion.3, bf16[512,512]{1,0:T(8,128)(2,1)S(1)} %copy.159, bf16[]{:T(256)} %constant.37.clone.1), kind=kCustom, calls=%fused_computation.92 | custom fusion | bytes 1048578 | tf_op jit(solution)/shard_map/scatter | solution.py:133
  152.7 4.6 %all-to-all-start.2 = ((bf16[128,8,512]{2,1,0:T(8,128)(2,1)}), bf16[128,8,512]{2,1,0:T(8,128)(2,1)S(1)}, u32[]{:S(2)}, u32[]{:S(2)}) async-start(bf16[128,8,512]{2,1,0:T(8,128)(2,1)} %bitcast.27), calls=%async_computation.2 | async-start | bytes 2097152 | tf_op jit(solution)/shard_map/all_to_all | solution.py:134
  159.0 17.7 %all-to-all-done.2 = bf16[128,8,512]{2,1,0:T(8,128)(2,1)S(1)} async-done(((bf16[128,8,512]{2,1,0:T(8,128)(2,1)}), bf16[128,8,512]{2,1,0:T(8,128)(2,1)S(1)}, u32[]{:S(2)}, u32[]{:S(2)}) %all-to-all-start.2) | async-done | bytes 1048608 | tf_op jit(solution)/shard_map/all_to_all | solution.py:134
  177.8 40.7 %all-gather.2.cloned.1.call-done = bf16[3072,512]{1,0:T(8,128)(2,1)} async-done(((bf16[96,512]{1,0:T(8,128)(2,1)}), bf16[3072,512]{1,0:T(8,128)(2,1)}) %all-gather.2.cloned.1.call-update) | async-done | bytes 3145744 | tf_op jit(solution)/shard_map/all_gather | solution.py:153
  218.5 5.5 %fusion.40 = bf16[384,512]{1,0:T(8,128)(2,1)} fusion(bf16[3072,512]{1,0:T(8,128)(2,1)} %all-gather.2.cloned.1.call-done, s32[384,3072]{1,0:T(8,128)} %param.14, s32[3072]{0:T(1024)S(1)} %iota_add_fusion, s32[384]{0:T(512)S(1)} %iota_add_fusion.2), kind=kOutput, calls=%fused_computation.64 | convolution fusion | flops 1212874752 | bytes 8271360 | tf_op jit(solution)/shard_map/dot_general | solution.py:158
  224.0 41.7 %all-reduce.2.cloned.1.call-done = bf16[384,512]{1,0:T(8,128)(2,1)} async-done(((bf16[384,512]{1,0:T(8,128)(2,1)}), bf16[384,512]{1,0:T(8,128)(2,1)}) %all-reduce.2.cloned.1.call-update) | async-done | bytes 393232 | tf_op jit(solution)/shard_map/psum | solution.py:159
  (97 shorter events, 35.7 us)
Async XLA Ops:
  6.5 261.6 %copy-start = (bf16[1024,512]{1,0:T(8,128)(2,1)S(1)}, bf16[1024,512]{1,0:T(8,128)(2,1)}, u32[]{:S(2)}) copy-start(bf16[1024,512]{1,0:T(8,128)(2,1)} %param.21) | copy-start | bytes 3145732
  6.5 38.9 %copy-start.1 = (bf16[96,512]{1,0:T(8,128)(2,1)S(1)}, bf16[96,512]{1,0:T(8,128)(2,1)}, u32[]{:S(2)}) copy-start(bf16[96,512]{1,0:T(8,128)(2,1)} %param.11) | copy-start | bytes 294916
  49.4 6.1 %copy-start.5 = (f32[2,16]{1,0:T(2,128)S(1)}, f32[2,16]{1,0:T(2,128)}, u32[]{:S(2)}) copy-start(f32[2,16]{1,0:T(2,128)} %param.18) | copy-start | bytes 388
  50.6 24.0 %all-to-all-start.1 = ((bf16[128,8,512]{2,1,0:T(8,128)(2,1)}), bf16[128,8,512]{2,1,0:T(8,128)(2,1)S(1)}, u32[]{:S(2)}, u32[]{:S(2)}) async-start(bf16[128,8,512]{2,1,0:T(8,128)(2,1)} %bitcast_select_fusion), calls=%async_computation.1 | async-start | bytes 2097152 | tf_op jit(solution)/shard_map/all_to_all | solution.py:127
  74.6 2.4 copy-start.8
  88.5 1.9 copy-start.2
  109.8 3.9 %copy-start.7 = (bf16[2,512,256]{2,1,0:T(8,128)(2,1)S(1)}, bf16[2,512,256]{2,1,0:T(8,128)(2,1)}, u32[]{:S(2)}) copy-start(bf16[2,512,256]{2,1,0:T(8,128)(2,1)} %param.16) | copy-start | bytes 1572868
  109.8 4.5 %copy-start.3 = (bf16[2,512,2048]{2,1,0:T(8,128)(2,1)S(1)}, bf16[2,512,2048]{2,1,0:T(8,128)(2,1)}, u32[]{:S(2)}) copy-start(bf16[2,512,2048]{2,1,0:T(8,128)(2,1)} %param.15) | copy-start | bytes 12582916
  113.4 0.8 copy-start.4
  152.7 24.0 %all-to-all-start.2 = ((bf16[128,8,512]{2,1,0:T(8,128)(2,1)}), bf16[128,8,512]{2,1,0:T(8,128)(2,1)S(1)}, u32[]{:S(2)}, u32[]{:S(2)}) async-start(bf16[128,8,512]{2,1,0:T(8,128)(2,1)} %bitcast.27), calls=%async_computation.2 | async-start | bytes 2097152 | tf_op jit(solution)/shard_map/all_to_all | solution.py:134
  157.4 61.2 %all-gather.2.cloned.1.call-start = ((), (), s32[]{:S(2)}) async-start(), calls=%async_computation.3 | async-start | bytes 3244032 | tf_op jit(solution)/shard_map/all_gather | solution.py:153
  177.7 88.0 %all-reduce.2.cloned.1.call-start = ((), (), s32[]{:S(2)}) async-start(), calls=%async_computation.4 | async-start | bytes 786432 | tf_op jit(solution)/shard_map/psum | solution.py:159
  177.8 90.4 %copy-start.6 = (bf16[512,1024]{1,0:T(8,128)(2,1)S(1)}, bf16[512,1024]{1,0:T(8,128)(2,1)}, u32[]{:S(2)}) copy-start(bf16[512,1024]{1,0:T(8,128)(2,1)} %param.20) | copy-start | bytes 3145732
Sparse Core Ops, SparseCore 0:
  177.8 40.6 all-gather.1
  224.2 41.5 all-reduce.1
where the time goes:
time: 279 us; the launch traced here: 278 us
  waiting for transfers between devices  119 us (43%)
  local copies, waits for them, and re-layouts  53.7 us (19%)
  matrix products  38.5 us (14%)
  other arithmetic  22.7 us (8%)
  blocking collectives  20.5 us (7%)
  between operations  13.8 us (5%)
  starting transfers between devices  9.52 us (3%)
    psum x1, waiting for transfers between devices, per_device(): lax.psum(neighbour_sum.astype(jnp.bfloat16), 'row').astype(jnp.float32)  41.7 us
    all_gather x1, waiting for transfers between devices, per_device(): piece = lax.all_gather(update, 'col', axis=0, tiled=True)  40.7 us
    all_to_all x1, blocking collectives, per_device(): lax.all_to_all(wanted.reshape(devices_all, capacity), ('row', 'col'), spl...  20.5 us
    all_to_all x1, waiting for transfers between devices, per_device(): lax.all_to_all(picked, ('row', 'col'), split_axis=0, concat_axis=0, tiled...  19.1 us
    all_to_all x1, waiting for transfers between devices, per_device(): lax.all_to_all(outgoing.reshape(devices_all, capacity, width), ('row', 'c...  17.7 us
    dot_general x2, matrix products, encode_walks(): jnp.einsum('whts,wshp->wthp', mix, inner, preferred_element_type=jnp.floa...  12.9 us
    another operation x2, other arithmetic, encode_walks(): running = jnp.transpose(jnp.cumsum(log_decay, axis=1), (0, 2, 1))  12.7 us
    transpose x2, local copies, waits for them, and re-layouts, encode_walks(): jnp.einsum('whts,wshp->wthp', mix, inner, preferred_element_type=jnp.floa...  11.2 us
  transfers between devices with their start and end apart: 4, of which 4 were waited for; matrix products, arithmetic and copies ran while one was open for 1% of the time, Pallas kernels for 0%

commit v1 on v0

--- a/solution.py
+++ b/solution.py
@@ -156,7 +156,9 @@
     self_link = (row_global[:, None] == col_global[None, :]).astype(jnp.int32)
     links = (adjacency + self_link).astype(jnp.bfloat16)
     neighbour_sum = jnp.dot(links, piece, preferred_element_type=jnp.float32)
-    combined = lax.psum(neighbour_sum.astype(jnp.bfloat16), "row").astype(jnp.float32)
+    combined = jnp.sum(lax.all_gather(neighbour_sum.astype(jnp.bfloat16), "row"), axis=0).astype(
+        jnp.float32
+    )
     return finish_nodes(combined, w_up, w_down)
 
 

time: 279 us -> 262 us (0.939)
  waiting for transfers between devices: 119 us -> 103 us
    psum x1 -> x0, waiting for transfers between devices: 41.7 us -> none  [per_device(): lax.psum(neighbour_sum.astype(jnp.bfloat16), 'row').astype(jnp.float32)]
    all_gather x0 -> x1, waiting for transfers between devices: none -> 25.8 us  [per_device(): lax.all_gather(neighbour_sum.astype(jnp.bfloat16), 'row')]
where the time goes in v1:
time: 262 us; the launch traced here: 261 us
  waiting for transfers between devices  103 us (39%)
  local copies, waits for them, and re-layouts  53.7 us (20%)
  matrix products  37.4 us (14%)
  other arithmetic  22.6 us (9%)
  blocking collectives  20.5 us (8%)
  between operations  13.8 us (5%)
  starting transfers between devices  9.52 us (4%)
    all_gather x1, waiting for transfers between devices, per_device(): piece = lax.all_gather(update, 'col', axis=0, tiled=True)  40.8 us
    all_gather x1, waiting for transfers between devices, per_device(): lax.all_gather(neighbour_sum.astype(jnp.bfloat16), 'row')  25.8 us
    all_to_all x1, blocking collectives, per_device(): lax.all_to_all(wanted.reshape(devices_all, capacity), ('row', 'col'), spl...  20.5 us
    all_to_all x1, waiting for transfers between devices, per_device(): lax.all_to_all(picked, ('row', 'col'), split_axis=0, concat_axis=0, tiled...  19.1 us
    all_to_all x1, waiting for transfers between devices, per_device(): lax.all_to_all(outgoing.reshape(devices_all, capacity, width), ('row', 'c...  17.7 us
    dot_general x2, matrix products, encode_walks(): jnp.einsum('whts,wshp->wthp', mix, inner, preferred_element_type=jnp.floa...  12.9 us
    another operation x2, other arithmetic, encode_walks(): running = jnp.transpose(jnp.cumsum(log_decay, axis=1), (0, 2, 1))  12.7 us
    transpose x2, local copies, waits for them, and re-layouts, encode_walks(): jnp.einsum('whts,wshp->wthp', mix, inner, preferred_element_type=jnp.floa...  11.2 us
  transfers between devices with their start and end apart: 4, of which 4 were waited for; matrix products, arithmetic and copies ran while one was open for 1% of the time, Pallas kernels for 0%

profile of v1, /device:TPU:0, one launch (start us, length us, event | category | flops | bytes accessed | tf_op | source)
XLA Modules:
  0.0 261.0 jit_solution(1381012875512830730)
XLA Ops:
  8.4 3.8 %sort.17 = (s32[512]{0:T(512)}, s32[512]{0:T(512)S(1)}) sort(s32[512]{0:T(512)S(1)} %iota_add_fusion.1, s32[512]{0:T(512)S(1)} %iota.44), dimensions={0}, to_apply=%region_0.1 | sort | flops 4608 | bytes 8192 | tf_op jit(solution)/shard_map/jit(argsort)/sort | solution.py:105
  12.2 3.5 %gather_fusion = s32[512]{0:T(512)S(1)} fusion(s32[512]{0:T(512)S(1)} %get-tuple-element.8, s32[1024]{0:T(1024)S(1)} %pad_clamp_fusion.2), kind=kCustom, calls=%fused_computation | custom fusion | bytes 6144 | tf_op jit(solution)/shard_map/gather | solution.py:106
  16.1 3.3 %gather_fusion.1 = s32[512]{0:T(512)S(1)} fusion(s32[128]{0:T(128)S(1)} %sub.82, s32[1024]{0:T(1024)S(1)} %pad_clamp_fusion.1), kind=kCustom, calls=%fused_computation.1 | custom fusion | bytes 6144 | tf_op jit(solution)/shard_map/gather | solution.py:110
  24.5 20.5 %all_to_all.19 = s32[128,1,8]{2,1,0:T(1,128)S(1)} all-to-all(s32[128,1,8]{2,1,0:T(1,128)S(1)} %bitcast.86), channel_id=1, replica_groups=mesh['row'=4,'col'=32] {'row','col'}, dimensions={0} | all-to-all | bytes 8192 | tf_op jit(solution)/shard_map/all_to_all | solution.py:119
  45.4 4.0 %gather_fusion.2 = bf16[1024,512]{1,0:T(8,128)(2,1)S(1)} fusion(bf16[96,512]{1,0:T(8,128)(2,1)S(1)} %copy-done.1, s32[1024]{0:T(1024)S(1)} %broadcast_clamp_fusion), kind=kCustom, calls=%fused_computation.2 | custom fusion | bytes 2101248 | tf_op jit(solution)/shard_map/gather | solution.py:76
  50.6 4.8 %all-to-all-start.1 = ((bf16[128,8,512]{2,1,0:T(8,128)(2,1)}), bf16[128,8,512]{2,1,0:T(8,128)(2,1)S(1)}, u32[]{:S(2)}, u32[]{:S(2)}) async-start(bf16[128,8,512]{2,1,0:T(8,128)(2,1)} %bitcast_select_fusion), calls=%async_computation.1 | async-start | bytes 2097152 | tf_op jit(solution)/shard_map/all_to_all | solution.py:127
  55.5 19.1 %all-to-all-done.1 = bf16[128,8,512]{2,1,0:T(8,128)(2,1)S(1)} async-done(((bf16[128,8,512]{2,1,0:T(8,128)(2,1)}), bf16[128,8,512]{2,1,0:T(8,128)(2,1)S(1)}, u32[]{:S(2)}, u32[]{:S(2)}) %all-to-all-start.1) | async-done | bytes 1048608 | tf_op jit(solution)/shard_map/all_to_all | solution.py:127
  77.5 6.3 %fusion.112 = f32[8,64,16]{2,0,1:T(8,128)S(1)} fusion(f32[8,64,16]{2,0,1:T(8,128)S(1)} %copy.147), kind=kOutput, calls=%fused_computation.165 | output fusion | flops 516096 | bytes 65536 | tf_op jit(solution)/shard_map/jit(cumsum)/reduce_window_sum | solution.py:41
  92.9 6.4 %convolution_bitcast_fusion.1 = f32[8,64,16,64]{1,3,2,0:T(8,128)} fusion(bf16[8,64,16,64]{3,2,1,0:T(8,128)(2,1)} %reshape.227, f32[8,16,64]{2,1,0:T(8,128)S(1)} %copy.149, f32[8,16,64]{2,1,0:T(8,128)S(1)} %bitcast_subtract_fusion.1, f32[8,16,64]{2,1,0:T(8,128)S(1)} %bitcast.82, f32[8,64,64]{2,1,0:T(8,128)S(1)} %convolution_multiply_fusion.1, ...), kind=kOutput, calls=%fused_computation.15 | convolution fusion | flops 72351744 | bytes 3383296 | tf_op jit(solution)/shard_map/whts,wshp->wthp/dot_general | solution.py:54
  99.3 5.6 %copy.151 = f32[8,64,16,64]{3,2,1,0:T(8,128)} copy(f32[8,64,16,64]{1,3,2,0:T(8,128)} %convolution_bitcast_fusion.1) | data formatting | bytes 4194304 | tf_op jit(solution)/shard_map/whts,wshp->wthp/transpose | solution.py:54
  104.9 4.9 %reshape.230 = f32[512,1024]{1,0:T(8,128)} reshape(f32[8,64,16,64]{3,2,1,0:T(8,128)} %copy.151) | data formatting | bytes 4194304 | tf_op jit(solution)/shard_map/reshape | solution.py:55
  109.8 3.6 %fusion.46 = (f32[512]{0:T(512)S(1)}, bf16[512,512]{0,1:T(8,128)(2,1)S(1)}) fusion(bf16[2,1024,512]{2,1,0:T(8,128)(2,1)} %param.19, f32[512,1024]{1,0:T(8,128)} %reshape.230, f32[512,2048]{1,0:T(8,128)} %copy-done.2, bf16[512,512]{0,1:T(8,128)(2,1)S(1)} %copy.145), kind=kOutput, calls=%fused_computation.75 | convolution fusion | flops 541588992 | bytes 6293504 | tf_op jit(solution)/shard_map/dot_general | solution.py:58
  114.3 3.2 %fusion.3 = f32[512,2048]{1,0:T(8,128)} fusion(bf16[2,512,2048]{2,1,0:T(8,128)(2,1)S(1)} %copy-done.3, bf16[512,512]{0,1:T(8,128)(2,1)S(1)} %get-tuple-element.14, f32[512]{0:T(512)S(1)} %add_rsqrt_fusion.1), kind=kOutput, calls=%fused_computation.18 | convolution fusion | flops 1074528256 | bytes 6817792 | tf_op jit(solution)/shard_map/dot_general | solution.py:23
  117.8 6.3 %fusion.113 = f32[8,64,16]{2,0,1:T(8,128)S(1)} fusion(f32[8,64,16]{2,0,1:T(8,128)S(1)} %copy.153), kind=kOutput, calls=%fused_computation.166 | output fusion | flops 516096 | bytes 65536 | tf_op jit(solution)/shard_map/jit(cumsum)/reduce_window_sum | solution.py:41
  128.7 6.4 %convolution_bitcast_fusion = f32[8,64,16,64]{1,3,2,0:T(8,128)} fusion(bf16[8,64,16,64]{3,2,1,0:T(8,128)(2,1)} %reshape.231, f32[8,16,64]{2,1,0:T(8,128)S(1)} %copy.155, f32[8,16,64]{2,1,0:T(8,128)S(1)} %bitcast_subtract_fusion, f32[8,16,64]{2,1,0:T(8,128)S(1)} %bitcast.83, f32[8,64,64]{2,1,0:T(8,128)S(1)} %convolution_multiply_fusion, ...), kind=kOutput, calls=%fused_computation.14 | convolution fusion | flops 72351744 | bytes 3383296 | tf_op jit(solution)/shard_map/whts,wshp->wthp/dot_general | solution.py:54
  135.1 5.6 %copy.157 = f32[8,64,16,64]{3,2,1,0:T(8,128)} copy(f32[8,64,16,64]{1,3,2,0:T(8,128)} %convolution_bitcast_fusion) | data formatting | bytes 4194304 | tf_op jit(solution)/shard_map/whts,wshp->wthp/transpose | solution.py:54
  140.7 3.5 %reshape.234 = f32[512,1024]{1,0:T(8,128)S(1)} reshape(f32[8,64,16,64]{3,2,1,0:T(8,128)} %copy.157) | data formatting | bytes 4194304 | tf_op jit(solution)/shard_map/reshape | solution.py:55
  144.2 3.8 %fusion.41 = bf16[512,512]{0,1:T(8,128)(2,1)} fusion(bf16[512,512]{0,1:T(8,128)(2,1)} %copy-done.4, bf16[2,1024,512]{2,1,0:T(8,128)(2,1)} %param.19, f32[512,1024]{1,0:T(8,128)S(1)} %reshape.234, f32[512,2048]{1,0:T(8,128)} %fusion.3, pred[512]{0:T(512)(128)(4,1)S(1)} %lt.51), kind=kOutput, calls=%fused_computation.65 | convolution fusion | flops 541065216 | bytes 6291968 | tf_op jit(solution)/shard_map/dot_general | solution.py:58
  149.2 3.5 %scatter_custom_fusion.2 = bf16[1024,512]{1,0:T(8,128)(2,1)} fusion(s32[512]{0:T(512)S(1)} %compare_select_fusion.3, bf16[512,512]{1,0:T(8,128)(2,1)S(1)} %copy.159, bf16[]{:T(256)} %constant.39.clone.1), kind=kCustom, calls=%fused_computation.92 | custom fusion | bytes 1048578 | tf_op jit(solution)/shard_map/scatter | solution.py:133
  152.7 4.6 %all-to-all-start.2 = ((bf16[128,8,512]{2,1,0:T(8,128)(2,1)}), bf16[128,8,512]{2,1,0:T(8,128)(2,1)S(1)}, u32[]{:S(2)}, u32[]{:S(2)}) async-start(bf16[128,8,512]{2,1,0:T(8,128)(2,1)} %bitcast.27), calls=%async_computation.2 | async-start | bytes 2097152 | tf_op jit(solution)/shard_map/all_to_all | solution.py:134
  159.0 17.7 %all-to-all-done.2 = bf16[128,8,512]{2,1,0:T(8,128)(2,1)S(1)} async-done(((bf16[128,8,512]{2,1,0:T(8,128)(2,1)}), bf16[128,8,512]{2,1,0:T(8,128)(2,1)S(1)}, u32[]{:S(2)}, u32[]{:S(2)}) %all-to-all-start.2) | async-done | bytes 1048608 | tf_op jit(solution)/shard_map/all_to_all | solution.py:134
  177.8 40.8 %all-gather.4.cloned.1.call-done = bf16[3072,512]{1,0:T(8,128)(2,1)} async-done(((bf16[96,512]{1,0:T(8,128)(2,1)}), bf16[3072,512]{1,0:T(8,128)(2,1)}) %all-gather.4.cloned.1.call-update) | async-done | bytes 3145744 | tf_op jit(solution)/shard_map/all_gather | solution.py:153
  218.5 5.5 %fusion.40 = bf16[384,512]{1,0:T(8,128)(2,1)} fusion(bf16[3072,512]{1,0:T(8,128)(2,1)} %all-gather.4.cloned.1.call-done, s32[384,3072]{1,0:T(8,128)} %param.14, s32[3072]{0:T(1024)S(1)} %iota_add_fusion, s32[384]{0:T(512)S(1)} %iota_add_fusion.2), kind=kOutput, calls=%fused_computation.64 | convolution fusion | flops 1212874752 | bytes 8271360 | tf_op jit(solution)/shard_map/dot_general | solution.py:158
  224.0 25.8 %all-gather.6.cloned.1.call-done = bf16[1536,512]{1,0:T(8,128)(2,1)} async-done(((bf16[384,512]{1,0:T(8,128)(2,1)}), bf16[1536,512]{1,0:T(8,128)(2,1)}) %all-gather.6.cloned.1.call-update) | async-done | bytes 1572880 | tf_op jit(solution)/shard_map/all_gather | solution.py:159
  (98 shorter events, 34.5 us)
Async XLA Ops:
  6.5 245.6 %copy-start = (bf16[1024,512]{1,0:T(8,128)(2,1)S(1)}, bf16[1024,512]{1,0:T(8,128)(2,1)}, u32[]{:S(2)}) copy-start(bf16[1024,512]{1,0:T(8,128)(2,1)} %param.21) | copy-start | bytes 3145732
  6.5 38.9 %copy-start.1 = (bf16[96,512]{1,0:T(8,128)(2,1)S(1)}, bf16[96,512]{1,0:T(8,128)(2,1)}, u32[]{:S(2)}) copy-start(bf16[96,512]{1,0:T(8,128)(2,1)} %param.11) | copy-start | bytes 294916
  49.4 6.1 %copy-start.5 = (f32[2,16]{1,0:T(2,128)S(1)}, f32[2,16]{1,0:T(2,128)}, u32[]{:S(2)}) copy-start(f32[2,16]{1,0:T(2,128)} %param.18) | copy-start | bytes 388
  50.6 24.0 %all-to-all-start.1 = ((bf16[128,8,512]{2,1,0:T(8,128)(2,1)}), bf16[128,8,512]{2,1,0:T(8,128)(2,1)S(1)}, u32[]{:S(2)}, u32[]{:S(2)}) async-start(bf16[128,8,512]{2,1,0:T(8,128)(2,1)} %bitcast_select_fusion), calls=%async_computation.1 | async-start | bytes 2097152 | tf_op jit(solution)/shard_map/all_to_all | solution.py:127
  74.6 2.4 copy-start.8
  88.5 1.9 copy-start.2
  109.8 3.9 %copy-start.7 = (bf16[2,512,256]{2,1,0:T(8,128)(2,1)S(1)}, bf16[2,512,256]{2,1,0:T(8,128)(2,1)}, u32[]{:S(2)}) copy-start(bf16[2,512,256]{2,1,0:T(8,128)(2,1)} %param.16) | copy-start | bytes 1572868
  109.8 4.5 %copy-start.3 = (bf16[2,512,2048]{2,1,0:T(8,128)(2,1)S(1)}, bf16[2,512,2048]{2,1,0:T(8,128)(2,1)}, u32[]{:S(2)}) copy-start(bf16[2,512,2048]{2,1,0:T(8,128)(2,1)} %param.15) | copy-start | bytes 12582916
  113.4 0.8 copy-start.4
  152.7 24.0 %all-to-all-start.2 = ((bf16[128,8,512]{2,1,0:T(8,128)(2,1)}), bf16[128,8,512]{2,1,0:T(8,128)(2,1)S(1)}, u32[]{:S(2)}, u32[]{:S(2)}) async-start(bf16[128,8,512]{2,1,0:T(8,128)(2,1)} %bitcast.27), calls=%async_computation.2 | async-start | bytes 2097152 | tf_op jit(solution)/shard_map/all_to_all | solution.py:134
  157.4 61.2 %all-gather.4.cloned.1.call-start = ((), (), s32[]{:S(2)}) async-start(), calls=%async_computation.3 | async-start | bytes 3244032 | tf_op jit(solution)/shard_map/all_gather | solution.py:153
  177.7 72.2 %all-gather.6.cloned.1.call-start = ((), (), s32[]{:S(2)}) async-start(), calls=%async_computation.4 | async-start | bytes 1966080 | tf_op jit(solution)/shard_map/all_gather | solution.py:159
  224.0 28.1 %copy-start.6 = (bf16[512,1024]{1,0:T(8,128)(2,1)S(1)}, bf16[512,1024]{1,0:T(8,128)(2,1)}, u32[]{:S(2)}) copy-start(bf16[512,1024]{1,0:T(8,128)(2,1)} %param.20) | copy-start | bytes 3145732
Sparse Core Ops, SparseCore 0:
  177.8 40.6 all-gather.3
  224.2 25.6 all-gather.5
